TPU v7x, 256 devices: a whole 4x4x8 slice. The times are simulated.
256 devices in a mesh: slot: 8 (over y_lo, x), feat: 32 (over y_hi, z, core).
Axes of the slice: x: 4, y: 4 (y_hi: 2, y_lo: 2; y = y_hi * 2 + y_lo), z: 8, core: 2. Of those that a mesh axis runs over, the one named last changes fastest.
Arguments:
- acts_in: bfloat16 [3, 256, 2304], P(None, None, 'slot'), may hold values from -6 to 6
- acts_out: bfloat16 [3, 256, 2304], P(None, None, 'slot'), may hold values from -6 to 6
- enc_weight: bfloat16 [3, 2304, 16384], P(None, 'slot', 'feat'), may hold values from -0.125 to 0.125
- enc_bias: float32 [3, 16384], P(None, 'feat'), may hold values from -3 to 3
- dec_weight: bfloat16 [6, 16384, 2304], P(None, 'feat', 'slot'), may hold values from -0.046875 to 0.046875
- dec_bias: float32 [3, 2304], P(None, 'slot'), may hold values from -3 to 3
Outputs:
- enc_grad: float32 [3, 2304, 16384], P(None, 'slot', 'feat')
- enc_bias_grad: float32 [3, 16384], P(None, 'feat')
- dec_grad: float32 [6, 16384, 2304], P(None, 'feat', 'slot')
- mse: float32 [], replicated
All inputs are finite; a program needn't handle non-finite values.
Results may differ from a plain program's by a relative error of at most 0.0095.
Values may be sent and summed in bfloat16 or wider, within the bound.
No kernel may reach another device: no remote copies, remote signals or barrier semaphores. Data moves between devices by JAX's collectives and lax.ppermute only.
A program may use at most 64 MiB of HBM per device.

v0:
```python
import functools
import jax
import jax.numpy as jnp
from jax import lax
from jax.sharding import Mesh
from jax.sharding import PartitionSpec as P

D = 2304
SLOT = ("slot_0", "slot_1")
FEAT = ("feat_0", "feat_1", "feat_2")
SLOT_FEAT = ("slot_0", "slot_1", "feat_0", "feat_1", "feat_2")


def cut_along(x, dim, devices):
    before, after = (x.shape[:dim], x.shape[dim + 1 :])
    return jnp.moveaxis(x.reshape(*before, devices, -1, *after), dim, 0)


def sum_at_owner(x, axis, dim):
    tiles = cut_along(x, dim, lax.axis_size(axis))
    arrived = lax.all_to_all(tiles, axis, split_axis=0, concat_axis=0, tiled=True)
    return arrived.sum(axis=0)


def over_axes(x, axes):
    return functools.reduce(lax.psum, axes, x)


def sent_to_all(x, axis):
    devices = lax.axis_size(axis)
    return lax.all_to_all(jnp.broadcast_to(x[None], (devices, *x.shape)), axis, 0, 0, tiled=True)


def joined_along(tiles, dim):
    dims = list(tiles.shape[1:])
    dims[dim] *= tiles.shape[0]
    return jnp.moveaxis(tiles, 0, dim).reshape(dims)


def collect(x, axis, dim):
    tiles = sent_to_all(x, axis)
    return joined_along(tiles, dim)


def activate(preact):
    return (
        jnp.maximum(preact, 0.0).astype(jnp.bfloat16),
        jnp.where(preact > 0, 1.0, 0.0).astype(jnp.bfloat16),
    )


def local(acts_in, acts_out, enc_weight, enc_bias, dec_weight, dec_bias):
    layers = acts_in.shape[0]
    tokens = acts_in.shape[1]
    width_dev = acts_in.shape[2]
    feature_dev = enc_weight.shape[2]
    pair_list = [(a, b) for a in range(layers) for b in range(a, layers)]

    def encode_rows():
        pieces = [
            jnp.dot(acts_in[a], enc_weight[a], preferred_element_type=jnp.float32)
            for a in range(layers)
        ]
        return jnp.concatenate(pieces, axis=1)

    bias_row = enc_bias.reshape(1, layers * feature_dev)
    preact = lax.psum(encode_rows(), SLOT) + bias_row
    features, slopes = activate(preact)
    target = (
        jnp.transpose(acts_out, (1, 0, 2)).reshape(tokens, layers * width_dev).astype(jnp.float32)
    )
    dec_row = dec_bias.reshape(1, layers * width_dev)
    portion = tokens // lax.axis_size(FEAT)
    row_block = features
    pieces = []
    for decode_b in range(layers):
        summed = jnp.zeros((portion * lax.axis_size(FEAT), width_dev), jnp.float32)
        for decode_a in range(decode_b + 1):
            pair_num = pair_list.index((decode_a, decode_b))
            summed = summed + jnp.dot(
                row_block[:, decode_a * feature_dev : (decode_a + 1) * feature_dev],
                dec_weight[pair_num],
                preferred_element_type=jnp.float32,
            )
        pieces.append(summed)
    rebuilt = sum_at_owner(jnp.concatenate(pieces, axis=1), FEAT, 0)
    offset = lax.axis_index(FEAT) * portion
    error_full = rebuilt + dec_row - lax.dynamic_slice_in_dim(target, offset, portion, 0)
    squared = over_axes(jnp.sum(error_full * error_full), SLOT_FEAT)
    error_half = collect(error_full.astype(jnp.bfloat16), FEAT, 0)
    mse = squared / (layers * tokens * D)
    dec_grads = []
    for a, b in pair_list:
        dec_grads.append(
            lax.dot_general(
                features[:, a * feature_dev : (a + 1) * feature_dev],
                error_half[:, b * width_dev : (b + 1) * width_dev],
                (((0,), (0,)), ((), ())),
                preferred_element_type=jnp.float32,
            )
        )
    row_block = error_half
    partials = []
    for upstream_a in range(layers):
        summed = jnp.zeros((tokens, feature_dev), jnp.float32)
        for b in range(upstream_a, layers):
            pair_num = pair_list.index((upstream_a, b))
            summed = summed + lax.dot_general(
                row_block[:, b * width_dev : (b + 1) * width_dev],
                dec_weight[pair_num],
                (((1,), (1,)), ((), ())),
                preferred_element_type=jnp.float32,
            )
        partials.append(summed)
    upstream = lax.psum(jnp.concatenate(partials, axis=1), SLOT)
    delta = upstream * slopes.astype(jnp.float32)
    bias_grad = jnp.sum(delta, axis=0).reshape(layers, feature_dev)
    delta_half = delta.astype(jnp.bfloat16)
    enc_grads = []
    for a in range(layers):
        enc_grads.append(
            lax.dot_general(
                acts_in[a],
                delta_half[:, a * feature_dev : (a + 1) * feature_dev],
                (((0,), (0,)), ((), ())),
                preferred_element_type=jnp.float32,
            )
        )
    return (jnp.stack(enc_grads), bias_grad, jnp.stack(dec_grads), mse)


def solution(mesh):
    split = Mesh(
        mesh.devices.reshape(2, 4, 2, 8, 2), ("slot_0", "slot_1", "feat_0", "feat_1", "feat_2")
    )
    in_specs = (
        P(None, None, SLOT),
        P(None, None, SLOT),
        P(None, SLOT, FEAT),
        P(None, FEAT),
        P(None, FEAT, SLOT),
        P(None, SLOT),
    )
    out_specs = (P(None, SLOT, FEAT), P(None, FEAT), P(None, FEAT, SLOT), P())
    return jax.shard_map(local, mesh=split, in_specs=in_specs, out_specs=out_specs, check_vma=False)
```

profile of v0, /device:TPU:32, one launch (start us, length us, event | category | flops | bytes accessed | tf_op | source)
XLA Modules:
  0.0 258.0 jit_solution(12020248933589295281)
XLA Ops:
  7.2 1.4 fusion.26
  8.6 1.4 fusion.28
  9.9 1.4 fusion.30
  11.3 1.3 pad_maximum_fusion.1
  12.6 87.5 %all-reduce.3.cloned.1.call-done = f32[256,1536]{1,0:T(8,128)} async-done(((f32[256,1536]{1,0:T(8,128)}), f32[256,1536]{1,0:T(8,128)}) %all-reduce.3.cloned.1.call-update) | async-done | bytes 1572880 | tf_op jit(solution)/shard_map/psum | solution.py:67
  100.1 1.6 maximum_convert_fusion
  101.7 0.3 fusion.14
  101.9 0.3 fusion.20
  102.2 0.3 fusion.24
  102.5 0.3 convolution_add_fusion.4
  102.8 0.3 convolution_add_fusion.3
  103.0 0.3 convolution_add_fusion.5
  103.3 0.1 pad_maximum_fusion.3
  103.4 1.2 copy.15
  104.6 9.8 %all-to-all-start = ((f32[32,8,864]{2,1,0:T(8,128)}), f32[32,8,864]{2,1,0:T(8,128)S(1)}, u32[]{:S(2)}, u32[]{:S(2)}) async-start(f32[32,8,864]{2,1,0:T(8,128)} %bitcast.107), calls=%async_computation | async-start | bytes 1835008 | tf_op jit(solution)/shard_map/all_to_all | solution.py:21
  114.5 2.0 convert_element_type.33
  116.5 2.0 constant_dynamic-slice_fusion
  118.5 1.2 copy.17
  119.6 0.1 add.67
  119.7 22.4 %all-to-all-done = f32[32,8,864]{2,1,0:T(8,128)S(1)} async-done(((f32[32,8,864]{2,1,0:T(8,128)}), f32[32,8,864]{2,1,0:T(8,128)S(1)}, u32[]{:S(2)}, u32[]{:S(2)}) %all-to-all-start) | async-done | bytes 884768 | tf_op jit(solution)/shard_map/all_to_all | solution.py:21
  142.1 0.1 reduce_sum.27
  142.2 0.6 multiply_reduce_fusion
  142.8 21.1 %all_to_all.10 = bf16[32,8,864]{2,1,0:T(8,128)(2,1)S(1)} all-to-all(bf16[32,8,864]{2,1,0:T(8,128)(2,1)S(1)} %broadcast_in_dim.12), channel_id=1, replica_groups=mesh['slot_0'=2,'slot_1'=4,'feat_0'=2,'feat_1'=8,'feat_2'=2] {'feat_0','..., dimensions={0} | all-to-all | bytes 884736 | tf_op jit(solution)/shard_map/all_to_all | solution.py:31
  163.9 0.3 fusion.22
  164.2 0.3 fusion.16
  164.6 0.3 fusion.8
  164.9 0.3 convolution_add_fusion.2
  165.3 0.3 convolution_add_fusion.1
  165.6 0.3 convolution_add_fusion
  166.0 1.3 pad_maximum_fusion.2
  167.3 5.6 %psum.51 = f32[]{:T(128)} all-reduce(f32[]{:T(128)} %get-tuple-element.6), channel_id=1, replica_groups=mesh['slot_0'=2,'slot_1'=4,'feat_0'=2,'feat_1'=8,'feat_2'=2] {'slot_0'}, use_global_device_ids=true, to_apply=%region_5.6 | all-reduce | flops 1 | bytes 8 | tf_op jit(solution)/shard_map/psum | solution.py:26
  172.8 9.6 %psum.52 = f32[]{:T(128)} all-reduce(f32[]{:T(128)} %psum.51), channel_id=1, replica_groups=mesh['slot_0'=2,'slot_1'=4,'feat_0'=2,'feat_1'=8,'feat_2'=2] {'slot_1'}, use_global_device_ids=true, to_apply=%region_6.7 | all-reduce | flops 1 | bytes 8 | tf_op jit(solution)/shard_map/psum | solution.py:26
  182.5 7.1 %psum.53 = f32[]{:T(128)} all-reduce(f32[]{:T(128)} %psum.52), channel_id=1, replica_groups=mesh['slot_0'=2,'slot_1'=4,'feat_0'=2,'feat_1'=8,'feat_2'=2] {'feat_0'}, use_global_device_ids=true, to_apply=%region_7.8 | all-reduce | flops 1 | bytes 8 | tf_op jit(solution)/shard_map/psum | solution.py:26
  189.5 15.8 %psum.54 = f32[]{:T(128)} all-reduce(f32[]{:T(128)} %psum.53), channel_id=1, replica_groups=mesh['slot_0'=2,'slot_1'=4,'feat_0'=2,'feat_1'=8,'feat_2'=2] {'feat_1'}, use_global_device_ids=true, to_apply=%region_8.9 | all-reduce | flops 1 | bytes 8 | tf_op jit(solution)/shard_map/psum | solution.py:26
  205.3 3.1 %psum.55 = f32[]{:T(128)} all-reduce(f32[]{:T(128)} %psum.54), channel_id=1, replica_groups=mesh['slot_0'=2,'slot_1'=4,'feat_0'=2,'feat_1'=8,'feat_2'=2] {'feat_2'}, use_global_device_ids=true, to_apply=%region_9.10 | all-reduce | flops 1 | bytes 8 | tf_op jit(solution)/shard_map/psum | solution.py:26
  209.0 1.1 fusion.5
  210.1 1.2 fusion.4
  211.3 1.2 fusion.3
  212.6 1.2 fusion.2
  213.8 1.2 fusion.1
  215.0 1.2 fusion
  216.2 29.3 %all-reduce.5.cloned.1.call-done = f32[256,1536]{1,0:T(8,128)} async-done(((f32[256,1536]{1,0:T(8,128)}), f32[256,1536]{1,0:T(8,128)}) %all-reduce.5.cloned.1.call-update) | async-done | bytes 1572880 | tf_op jit(solution)/shard_map/psum | solution.py:115
  245.5 1.8 fusion.6
  247.3 0.2 convolution_bitcast_fusion
  247.5 0.2 convolution_bitcast_fusion.1
  247.8 0.2 convolution_bitcast_fusion.2
  248.0 0.6 reshape.27
  248.6 1.3 pad_maximum_fusion
  (16 shorter events, 0.2 us)
Async XLA Ops:
  7.2 92.9 %all-reduce.3.cloned.1.call-start = ((), (), s32[]{:S(2)}) async-start(), calls=%async_computation.2 | async-start | bytes 3145728 | tf_op jit(solution)/shard_map/psum | solution.py:67
  11.3 1.3 copy-start.3
  12.6 89.1 %copy-start = (bf16[6,512,288]{1,2,0:T(8,128)(2,1)S(1)}, bf16[6,512,288]{1,2,0:T(8,128)(2,1)}, u32[]{:S(2)}) copy-start(bf16[6,512,288]{1,2,0:T(8,128)(2,1)} %param.10) | copy-start | bytes 5308420
  104.6 37.5 %all-to-all-start = ((f32[32,8,864]{2,1,0:T(8,128)}), f32[32,8,864]{2,1,0:T(8,128)S(1)}, u32[]{:S(2)}, u32[]{:S(2)}) async-start(f32[32,8,864]{2,1,0:T(8,128)} %bitcast.107), calls=%async_computation | async-start | bytes 1835008 | tf_op jit(solution)/shard_map/all_to_all | solution.py:21
  114.4 5.2 %copy-start.4 = (f32[3,288]{1,0:T(4,128)S(1)}, f32[3,288]{1,0:T(4,128)}, u32[]{:S(2)}) copy-start(f32[3,288]{1,0:T(4,128)} %param.11) | copy-start | bytes 10372
  114.4 131.1 %all-reduce.5.cloned.1.call-start = ((), (), s32[]{:S(2)}) async-start(), calls=%async_computation.3 | async-start | bytes 3145728 | tf_op jit(solution)/shard_map/psum | solution.py:115
  212.6 33.0 %copy-start.1 = (f32[256,1536]{1,0:T(8,128)S(1)}, f32[256,1536]{1,0:T(8,128)}, u32[]{:S(2)}) copy-start(f32[256,1536]{1,0:T(8,128)} %all-reduce.3.cloned.1.call-done) | copy-start | bytes 4718596
  216.2 31.1 %copy-start.2 = (bf16[3,256,288]{1,2,0:T(8,128)(2,1)S(1)}, bf16[3,256,288]{1,2,0:T(8,128)(2,1)}, u32[]{:S(2)}) copy-start(bf16[3,256,288]{1,2,0:T(8,128)(2,1)} %param.6) | copy-start | bytes 1327108
Sparse Core Ops, SparseCore 0:
  12.7 87.3 all-reduce.2
  167.4 78.1 all-reduce.4
where the time goes:
time: 259 us; the launch traced here: 258 us
  waiting for transfers between devices  139 us (54%)
  blocking collectives  62.2 us (24%)
  between operations  16 us (6%)
  matrix products  15.5 us (6%)
  other arithmetic  9.89 us (4%)
  starting transfers between devices  9.88 us (4%)
  local copies, waits for them, and re-layouts  5.13 us (2%)
    psum x1, waiting for transfers between devices, local(): preact = lax.psum(encode_rows(), SLOT) + bias_row  87.5 us
    psum x5, blocking collectives, over_axes(): return functools.reduce(lax.psum, axes, x)  41.1 us
    psum x1, waiting for transfers between devices, local(): upstream = lax.psum(jnp.concatenate(partials, axis=1), SLOT)  29.3 us
    all_to_all x1, waiting for transfers between devices, sum_at_owner(): lax.all_to_all(tiles, axis, split_axis=0, concat_axis=0, tiled=True)  22.4 us
    all_to_all x1, blocking collectives, sent_to_all(): lax.all_to_all(jnp.broadcast_to(x[None], (devices, *x.shape)), axis, 0, 0...  21.1 us
    all_to_all x1, starting transfers between devices, sum_at_owner(): lax.all_to_all(tiles, axis, split_axis=0, concat_axis=0, tiled=True)  9.8 us
    dot_general x6, matrix products, local(): lax.dot_general(features[:, a * feature_dev:(a + 1) * feature_dev], error...  7.18 us
  transfers between devices with their start and end apart: 3, of which 3 were waited for; matrix products, arithmetic and copies ran while one was open for 5% of the time, Pallas kernels for 0%

commit v1 on v0

--- a/solution.py
+++ b/solution.py
@@ -9,6 +9,11 @@
 SLOT = ("slot_0", "slot_1")
 FEAT = ("feat_0", "feat_1", "feat_2")
 SLOT_FEAT = ("slot_0", "slot_1", "feat_0", "feat_1", "feat_2")
+
+
+def one_after_other(value, axis_one, axis_two):
+    partial = lax.psum(value, axis_one)
+    return lax.psum(partial, axis_two)
 
 
 def cut_along(x, dim, devices):
@@ -64,7 +69,7 @@
         return jnp.concatenate(pieces, axis=1)
 
     bias_row = enc_bias.reshape(1, layers * feature_dev)
-    preact = lax.psum(encode_rows(), SLOT) + bias_row
+    preact = one_after_other(encode_rows(), "slot_1", "slot_0") + bias_row
     features, slopes = activate(preact)
     target = (
         jnp.transpose(acts_out, (1, 0, 2)).reshape(tokens, layers * width_dev).astype(jnp.float32)

time: 259 us -> 296 us (1.14)
  waiting for transfers between devices: 139 us -> 176 us
    psum x1 -> x2, waiting for transfers between devices: 87.5 us -> 124 us  [the longest x1 65.9 us: one_after_other(): return lax.psum(partial, axis_two)]
  transfers between devices with their start and end apart: 3 -> 4, of which waited for: 3 -> 4; matrix products, arithmetic and copies ran while one was open for 5% -> 4% of each run, Pallas kernels for 0% -> 0%
where the time goes in v1:
time: 296 us
  waiting for transfers between devices  176 us (59%)
  blocking collectives  63.9 us (22%)
  between operations  15.7 us (5%)
  matrix products  15.5 us (5%)
  starting transfers between devices  9.91 us (3%)
  other arithmetic  9.89 us (3%)
  local copies, waits for them, and re-layouts  5.12 us (2%)
    psum x1, waiting for transfers between devices, one_after_other(): return lax.psum(partial, axis_two)  65.9 us
    psum x1, waiting for transfers between devices, one_after_other(): partial = lax.psum(value, axis_one)  58.3 us
    psum x5, blocking collectives, over_axes(): return functools.reduce(lax.psum, axes, x)  42.8 us
    psum x1, waiting for transfers between devices, local(): upstream = lax.psum(jnp.concatenate(partials, axis=1), SLOT)  29.1 us
    all_to_all x1, waiting for transfers between devices, sum_at_owner(): lax.all_to_all(tiles, axis, split_axis=0, concat_axis=0, tiled=True)  22.4 us
    all_to_all x1, blocking collectives, sent_to_all(): lax.all_to_all(jnp.broadcast_to(x[None], (devices, *x.shape)), axis, 0, 0...  21.1 us
    all_to_all x1, starting transfers between devices, sum_at_owner(): lax.all_to_all(tiles, axis, split_axis=0, concat_axis=0, tiled=True)  9.78 us
    dot_general x6, matrix products, local(): lax.dot_general(features[:, a * feature_dev:(a + 1) * feature_dev], error...  7.18 us
  transfers between devices with their start and end apart: 4, of which 4 were waited for; matrix products, arithmetic and copies ran while one was open for 4% of the time, Pallas kernels for 0%

profile of v1, /device:TPU:32, one launch (start us, length us, event | category | flops | bytes accessed | tf_op | source)
XLA Modules:
  0.0 295.8 jit_solution(13100654409273868253)
XLA Ops:
  7.2 1.4 fusion.26
  8.6 1.4 fusion.28
  9.9 1.4 fusion.30
  11.3 1.3 pad_maximum_fusion.1
  12.6 58.3 %all-reduce.4.cloned.1.call-done = f32[256,1536]{1,0:T(8,128)} async-done(((f32[256,1536]{1,0:T(8,128)}), f32[256,1536]{1,0:T(8,128)}) %all-reduce.4.cloned.1.call-update) | async-done | bytes 1572880 | tf_op jit(solution)/shard_map/psum | solution.py:15
  71.0 65.9 %all-reduce.6.cloned.1.call-done = f32[256,1536]{1,0:T(8,128)} async-done(((f32[256,1536]{1,0:T(8,128)}), f32[256,1536]{1,0:T(8,128)}) %all-reduce.6.cloned.1.call-update) | async-done | bytes 1572880 | tf_op jit(solution)/shard_map/psum | solution.py:16
  136.9 1.6 maximum_convert_fusion
  138.5 0.3 fusion.14
  138.7 0.3 fusion.20
  139.0 0.3 fusion.24
  139.3 0.3 convolution_add_fusion.4
  139.5 0.3 convolution_add_fusion.3
  139.8 0.3 convolution_add_fusion.5
  140.2 1.2 copy.15
  141.4 9.8 %all-to-all-start = ((f32[32,8,864]{2,1,0:T(8,128)}), f32[32,8,864]{2,1,0:T(8,128)S(1)}, u32[]{:S(2)}, u32[]{:S(2)}) async-start(f32[32,8,864]{2,1,0:T(8,128)} %bitcast.107), calls=%async_computation | async-start | bytes 1835008 | tf_op jit(solution)/shard_map/all_to_all | solution.py:26
  151.3 2.0 convert_element_type.33
  153.3 2.0 constant_dynamic-slice_fusion
  155.2 1.2 copy.17
  156.4 0.1 add.69
  156.5 22.4 %all-to-all-done = f32[32,8,864]{2,1,0:T(8,128)S(1)} async-done(((f32[32,8,864]{2,1,0:T(8,128)}), f32[32,8,864]{2,1,0:T(8,128)S(1)}, u32[]{:S(2)}, u32[]{:S(2)}) %all-to-all-start) | async-done | bytes 884768 | tf_op jit(solution)/shard_map/all_to_all | solution.py:26
  178.9 0.1 reduce_sum.27
  178.9 0.6 multiply_reduce_fusion
  179.6 21.1 %all_to_all.10 = bf16[32,8,864]{2,1,0:T(8,128)(2,1)S(1)} all-to-all(bf16[32,8,864]{2,1,0:T(8,128)(2,1)S(1)} %broadcast_in_dim.12), channel_id=1, replica_groups=mesh['slot_0'=2,'slot_1'=4,'feat_0'=2,'feat_1'=8,'feat_2'=2] {'feat_0','..., dimensions={0} | all-to-all | bytes 884736 | tf_op jit(solution)/shard_map/all_to_all | solution.py:36
  200.7 0.3 fusion.22
  201.0 0.3 fusion.16
  201.3 0.3 fusion.8
  201.7 0.3 convolution_add_fusion.2
  202.0 0.3 convolution_add_fusion.1
  202.4 0.3 convolution_add_fusion
  202.7 1.3 pad_maximum_fusion.2
  204.0 5.6 %psum.59 = f32[]{:T(128)} all-reduce(f32[]{:T(128)} %get-tuple-element.6), channel_id=1, replica_groups=mesh['slot_0'=2,'slot_1'=4,'feat_0'=2,'feat_1'=8,'feat_2'=2] {'slot_0'}, use_global_device_ids=true, to_apply=%region_6.7 | all-reduce | flops 1 | bytes 8 | tf_op jit(solution)/shard_map/psum | solution.py:31
  209.6 11.0 %psum.60 = f32[]{:T(128)} all-reduce(f32[]{:T(128)} %psum.59), channel_id=1, replica_groups=mesh['slot_0'=2,'slot_1'=4,'feat_0'=2,'feat_1'=8,'feat_2'=2] {'slot_1'}, use_global_device_ids=true, to_apply=%region_7.8 | all-reduce | flops 1 | bytes 8 | tf_op jit(solution)/shard_map/psum | solution.py:31
  220.6 7.1 %psum.61 = f32[]{:T(128)} all-reduce(f32[]{:T(128)} %psum.60), channel_id=1, replica_groups=mesh['slot_0'=2,'slot_1'=4,'feat_0'=2,'feat_1'=8,'feat_2'=2] {'feat_0'}, use_global_device_ids=true, to_apply=%region_8.9 | all-reduce | flops 1 | bytes 8 | tf_op jit(solution)/shard_map/psum | solution.py:31
  227.7 16.0 %psum.62 = f32[]{:T(128)} all-reduce(f32[]{:T(128)} %psum.61), channel_id=1, replica_groups=mesh['slot_0'=2,'slot_1'=4,'feat_0'=2,'feat_1'=8,'feat_2'=2] {'feat_1'}, use_global_device_ids=true, to_apply=%region_9.10 | all-reduce | flops 1 | bytes 8 | tf_op jit(solution)/shard_map/psum | solution.py:31
  243.7 3.1 %psum.63 = f32[]{:T(128)} all-reduce(f32[]{:T(128)} %psum.62), channel_id=1, replica_groups=mesh['slot_0'=2,'slot_1'=4,'feat_0'=2,'feat_1'=8,'feat_2'=2] {'feat_2'}, use_global_device_ids=true, to_apply=%region_10.11 | all-reduce | flops 1 | bytes 8 | tf_op jit(solution)/shard_map/psum | solution.py:31
  247.4 1.1 fusion.5
  248.5 1.2 fusion.4
  249.8 1.2 fusion.3
  251.0 1.2 fusion.2
  252.2 1.2 fusion.1
  253.4 1.2 fusion
  254.6 29.1 %all-reduce.8.cloned.1.call-done = f32[256,1536]{1,0:T(8,128)} async-done(((f32[256,1536]{1,0:T(8,128)}), f32[256,1536]{1,0:T(8,128)}) %all-reduce.8.cloned.1.call-update) | async-done | bytes 1572880 | tf_op jit(solution)/shard_map/psum | solution.py:120
  283.7 1.8 fusion.6
  285.5 0.2 convolution_bitcast_fusion
  285.7 0.2 convolution_bitcast_fusion.1
  286.0 0.2 convolution_bitcast_fusion.2
  286.2 0.6 reshape.27
  286.8 1.3 pad_maximum_fusion
  (19 shorter events, 0.3 us)
Async XLA Ops:
  7.2 63.8 %all-reduce.4.cloned.1.call-start = ((), (), s32[]{:S(2)}) async-start(), calls=%async_computation.2 | async-start | bytes 3145728 | tf_op jit(solution)/shard_map/psum | solution.py:15
  12.6 58.4 %copy-start.3 = (f32[3,512]{1,0:T(4,128)S(1)}, f32[3,512]{1,0:T(4,128)}, u32[]{:S(2)}) copy-start(f32[3,512]{1,0:T(4,128)} %param.9) | copy-start | bytes 18436
  12.6 124.3 %all-reduce.6.cloned.1.call-start = ((), (), s32[]{:S(2)}) async-start(), calls=%async_computation.3 | async-start | bytes 3145728 | tf_op jit(solution)/shard_map/psum | solution.py:16
  70.9 67.5 %copy-start = (bf16[6,512,288]{1,2,0:T(8,128)(2,1)S(1)}, bf16[6,512,288]{1,2,0:T(8,128)(2,1)}, u32[]{:S(2)}) copy-start(bf16[6,512,288]{1,2,0:T(8,128)(2,1)} %param.10) | copy-start | bytes 5308420
  141.4 37.5 %all-to-all-start = ((f32[32,8,864]{2,1,0:T(8,128)}), f32[32,8,864]{2,1,0:T(8,128)S(1)}, u32[]{:S(2)}, u32[]{:S(2)}) async-start(f32[32,8,864]{2,1,0:T(8,128)} %bitcast.107), calls=%async_computation | async-start | bytes 1835008 | tf_op jit(solution)/shard_map/all_to_all | solution.py:26
  151.2 5.2 %copy-start.4 = (f32[3,288]{1,0:T(4,128)S(1)}, f32[3,288]{1,0:T(4,128)}, u32[]{:S(2)}) copy-start(f32[3,288]{1,0:T(4,128)} %param.11) | copy-start | bytes 10372
  151.2 132.5 %all-reduce.8.cloned.1.call-start = ((), (), s32[]{:S(2)}) async-start(), calls=%async_computation.4 | async-start | bytes 3145728 | tf_op jit(solution)/shard_map/psum | solution.py:120
  251.0 32.7 %copy-start.1 = (f32[256,1536]{1,0:T(8,128)S(1)}, f32[256,1536]{1,0:T(8,128)}, u32[]{:S(2)}) copy-start(f32[256,1536]{1,0:T(8,128)} %all-reduce.6.cloned.1.call-done) | copy-start | bytes 4718596
  254.6 30.8 %copy-start.2 = (bf16[3,256,288]{1,2,0:T(8,128)(2,1)S(1)}, bf16[3,256,288]{1,2,0:T(8,128)(2,1)}, u32[]{:S(2)}) copy-start(bf16[3,256,288]{1,2,0:T(8,128)(2,1)} %param.6) | copy-start | bytes 1327108
Sparse Core Ops, SparseCore 0:
  12.7 58.1 all-reduce.3
  73.5 63.3 all-reduce.5
  204.1 79.5 all-reduce.7
